TPU v7x, 256 devices: a whole 4x4x8 slice. The times are simulated.
256 devices in a mesh: space: 32 (over y, z), frag: 8 (over x, core).
Axes of the slice: x: 4, y: 4, z: 8, core: 2. Of those that a mesh axis runs over, the one named last changes fastest.
Arguments:
- latents: bfloat16 [1048576, 128], P(('space', 'frag')), may hold values from -6 to 6
- positions: float32 [3, 1048576], P(None, ('space', 'frag')), may hold values from 0 to 12
- masses: float32 [1048576], P(('space', 'frag')), may hold values from 0.5 to 2
- w_value: bfloat16 [128, 128], replicated, may hold values from -0.5 to 0.5
- w_self: bfloat16 [128, 128], replicated, may hold values from -0.5 to 0.5
- w_message: bfloat16 [128, 128], replicated, may hold values from -0.5 to 0.5
- w_offset: float32 [3, 128], replicated, may hold values from -3.5 to 3.5
- bias_hidden: float32 [128], replicated, may hold values from -3 to 3
- w_out: bfloat16 [128, 128], replicated, may hold values from -0.5 to 0.5
- norm_gain: float32 [128], replicated, may hold values from 0.1 to 1.9
- tile_blocks: int32 [2, 163840], P(None, ('space', 'frag')), may hold values from 0 to 39, as said below
- tile_count: int32 [256], P(('space', 'frag')), may hold values from 80 to 640, as said below
- send_rows: int32 [4, 65536], P(None, ('space', 'frag')), may hold values from 0 to 4095
- frag_ids: int32 [1048576], P(('space', 'frag')), may hold values from 0 to 1023
Outputs:
- updated: bfloat16 [1048576, 128], P(('space', 'frag'))
- pooled: float32 [1024, 128], P('frag')
Inputs may be any that keep to these rules, and one draw needn't show every extreme that they name: `tile_blocks`: row 0 names a block of the device's own 32 blocks; row 1 names one of the 40 blocks of the extended rows. Only the first tile_count slots of a device are live; some device has all 640 live.
All inputs are finite; a program needn't handle non-finite values.
Results may differ from a plain program's by a relative error of at most 0.012.
Values may be sent and summed in bfloat16 or wider, within the bound.
A program may use at most 64 MiB of HBM per device.

v0:
```python
import math
import jax
import jax.numpy as jnp
from jax import lax
from jax.sharding import PartitionSpec as P

D = 128
TILE = 128
GROUP = 32
REACH = 2
FR_DEV = 128
norm_eps = 1e-05


def passed_along(value, axis, by):
    size = lax.axis_size(axis)
    pairs = [(i, i + by) for i in range(size) if 0 <= i + by < size]
    return lax.ppermute(value, axis, pairs)


def offsets_list():
    return [shift_by for shift_by in range(-REACH, REACH + 1) if shift_by != 0]


def tile_terms(running, group_id, blocks, live_tiles, ext_values, ext_pos, ext_mass, recv_blocks):
    message, moment, weight_sum = running
    first_slot = group_id * GROUP
    tile_index = first_slot + jnp.arange(GROUP, dtype=jnp.int32)
    receiver = lax.dynamic_slice_in_dim(blocks[0], first_slot, GROUP, 0)
    sender = lax.dynamic_slice_in_dim(blocks[1], first_slot, GROUP, 0)
    active = (tile_index < live_tiles).astype(jnp.float32)
    recv_pos = recv_blocks[receiver]
    send_pos = ext_pos[sender]
    squared = jnp.zeros((GROUP, TILE, TILE), jnp.float32)
    for c in range(3):
        delta = recv_pos[:, c, :, None] - send_pos[:, c, None, :]
        squared = squared + delta * delta
    distance = jnp.sqrt(squared)
    weight = (ext_mass[sender] * active[:, None])[:, None, :] * jnp.exp(-distance)
    terms = jnp.einsum(
        "gij,gjd->gid",
        weight.astype(jnp.bfloat16),
        ext_values[sender],
        preferred_element_type=jnp.float32,
    )
    message = message.at[receiver].add(terms)
    moment = moment.at[receiver].add(
        jnp.einsum("gij,gcj->gci", weight, send_pos, precision=lax.Precision.HIGHEST)
    )
    weight_sum = weight_sum.at[receiver].add(jnp.sum(weight, axis=2))
    return (message, moment, weight_sum)


def node_update(
    own_latents,
    own_pos,
    message,
    moment,
    weight_sum,
    w_self,
    w_message,
    w_offset,
    bias_hidden,
    w_out,
    norm_gain,
):
    rows = own_latents.shape[0]
    flat_sum = weight_sum.reshape(rows)
    aggregated = (message.reshape(rows, D) * lax.rsqrt(flat_sum)[:, None]).astype(jnp.bfloat16)
    centre = moment.transpose(1, 0, 2).reshape(3, rows) / flat_sum[None, :] - own_pos
    hidden_pre = jnp.dot(own_latents, w_self, preferred_element_type=jnp.float32)
    hidden_pre = hidden_pre + jnp.dot(aggregated, w_message, preferred_element_type=jnp.float32)
    for c in range(3):
        hidden_pre = hidden_pre + centre[c][:, None] * w_offset[c][None, :]
    hidden = jax.nn.silu(hidden_pre + bias_hidden[None, :]).astype(jnp.bfloat16)
    projected = jnp.dot(hidden, w_out, preferred_element_type=jnp.float32)
    row_mean = jnp.mean(projected, axis=1, keepdims=True)
    centred = projected - row_mean
    row_var = jnp.mean(centred * centred, axis=1, keepdims=True)
    normed = centred * lax.rsqrt(row_var + norm_eps) * norm_gain[None, :]
    return (own_latents.astype(jnp.float32) + normed).astype(jnp.bfloat16)


def shards(
    latents,
    positions,
    masses,
    w_value,
    w_self,
    w_message,
    w_offset,
    bias_hidden,
    w_out,
    norm_gain,
    tile_blocks,
    tile_count,
    send_rows,
    frag_ids,
):
    own_rows = latents.shape[0]
    num_blocks = own_rows // TILE
    values = jnp.dot(latents, w_value, preferred_element_type=jnp.float32).astype(jnp.bfloat16)
    shifts_by = offsets_list()
    send_values = values[send_rows]
    send_pos = positions[:, send_rows].transpose(1, 0, 2)
    send_mass = masses[send_rows]
    arrived_by_slot = {}
    for k, shift_by in enumerate(shifts_by):
        arrived_by_slot[k] = (
            passed_along(send_values[k], "space", shift_by),
            passed_along(send_pos[k].astype(jnp.bfloat16), "space", shift_by).astype(jnp.float32),
            passed_along(send_mass[k].astype(jnp.bfloat16), "space", shift_by).astype(jnp.float32),
        )
    halo_values = [values] + [arrived_by_slot[k][0] for k in range(len(shifts_by))]
    halo_pos = [positions] + [arrived_by_slot[k][1] for k in range(len(shifts_by))]
    halo_mass = [masses] + [arrived_by_slot[k][2] for k in range(len(shifts_by))]
    ext_values = jnp.concatenate(halo_values, 0).reshape(-1, TILE, D)
    ext_pos = jnp.concatenate(halo_pos, 1).reshape(3, -1, TILE).transpose(1, 0, 2)
    ext_mass = jnp.concatenate(halo_mass, 0).reshape(-1, TILE)
    recv_blocks = positions.reshape(3, num_blocks, TILE).transpose(1, 0, 2)
    live_tiles = tile_count[0]
    initial = (
        jnp.zeros((num_blocks, TILE, D), jnp.float32),
        recv_blocks * masses.reshape(num_blocks, 1, TILE),
        masses.reshape(num_blocks, TILE),
    )

    def advance(group_id, running):
        return tile_terms(
            running, group_id, tile_blocks, live_tiles, ext_values, ext_pos, ext_mass, recv_blocks
        )

    final = lax.fori_loop(0, tile_blocks.shape[1] // GROUP, advance, initial)
    message, moment, weight_sum = final
    updated = node_update(
        latents,
        positions,
        message,
        moment,
        weight_sum,
        w_self,
        w_message,
        w_offset,
        bias_hidden,
        w_out,
        norm_gain,
    )
    n_space = lax.axis_size("space")
    n_frag = lax.axis_size("frag")
    num_frags = FR_DEV * n_frag
    pool_scale = math.sqrt(num_frags / (own_rows * n_space * n_frag))
    partial_value = jax.ops.segment_sum(
        updated.astype(jnp.float32), frag_ids, num_segments=num_frags
    )
    summed = lax.psum(partial_value.astype(jnp.bfloat16), "space")
    pooled = lax.psum_scatter(summed, "frag", scatter_dimension=0, tiled=True).astype(jnp.float32)
    return (updated, pooled * pool_scale)


def solution(mesh):
    return jax.shard_map(
        shards,
        mesh=mesh,
        in_specs=(
            P(("space", "frag"), None),
            P(None, ("space", "frag")),
            P(("space", "frag")),
            P(),
            P(),
            P(),
            P(),
            P(),
            P(),
            P(),
            P(None, ("space", "frag")),
            P(("space", "frag")),
            P(None, ("space", "frag")),
            P(("space", "frag")),
        ),
        out_specs=(P(("space", "frag"), None), P("frag", None)),
        check_vma=False,
    )
```

profile of v0, /device:TPU:0, one launch (start us, length us, event | category | flops | bytes accessed | tf_op | source)
XLA Modules:
  0.0 1036.8 jit_solution(7022390476027426565)
XLA Ops:
  8.7 6.1 gather_fusion.4
  18.0 5.1 collective-permute-start.2
  23.1 5.4 collective-permute-start.3
  52.7 5.4 collective-permute-start.11
  60.7 5.4 collective-permute-done.4
  77.4 7.5 collective-permute-start.7
  87.0 727.9 %while.17 = (s32[]{:T(128)}, f32[32,128,128]{2,1,0:T(8,128)S(1)}, f32[32,3,128]{2,1,0:T(4,128)}, f32[32,128]{1,0:T(8,128)S(1)}, s32[2,640]{1,0:T(2,128)}, /*inde...) while((s32[]{:T(128)}, f32[32,128,128]{2,1,0:T(8,128)S(1)}, ...), condition=%wide.region_5.0_spmd, body=%wide.region_0.0_spmd.sunk | while | flops 170412320 | bytes 12668991 | solution.py:133
  108.2 6.2 fusion.74
  144.5 6.2 fusion.74
  180.9 6.2 fusion.74
  217.3 6.2 fusion.74
  253.7 6.2 fusion.74
  290.1 6.2 fusion.74
  326.5 6.2 fusion.74
  362.9 6.2 fusion.74
  399.3 6.2 fusion.74
  435.7 6.2 fusion.74
  467.4 4.7 scatter_fusion
  472.1 6.2 fusion.74
  508.5 6.2 fusion.74
  544.9 6.2 fusion.74
  576.6 4.7 scatter_fusion
  581.3 6.2 fusion.74
  617.7 6.2 fusion.74
  654.1 6.2 fusion.74
  690.5 6.2 fusion.74
  726.9 6.2 fusion.74
  763.3 6.2 fusion.74
  799.7 6.2 fusion.74
  823.1 23.2 %scatter_custom_fusion.3 = f32[1024,128]{1,0:T(8,128)} fusion(s32[4096]{0:T(1024)} %param.29, f32[4096,128]{1,0:T(8,128)S(1)} %copy.23, f32[]{:T(128)} %constant.62.clone.1), kind=kCustom, calls=%fused_computation.58 | custom fusion | flops 524288 | bytes 524800 | tf_op jit(solution)/shard_map/scatter-add | solution.py:152
  849.4 36.8 %reduce-scatter.2.cloned.1.call-done = bf16[128,128]{1,0:T(8,128)(2,1)} async-done(((bf16[1024,128]{1,0:T(8,128)(2,1)}), bf16[128,128]{1,0:T(8,128)(2,1)}) %reduce-scatter.2.cloned.1.call-update) | async-done | bytes 32784 | tf_op jit(solution)/shard_map/reduce_scatter | solution.py:156
  886.2 143.1 %psum.8 = bf16[128,128]{1,0:T(8,128)(2,1)S(1)} all-reduce(bf16[128,128]{1,0:T(8,128)(2,1)} %reduce-scatter.2.cloned.1.call-done), channel_id=1, replica_groups=mesh['space'=32,'frag'=8] {'space'}, use_global_device_ids=true, to_apply=%region_9.10 | all-reduce | flops 16384 | bytes 65536 | tf_op jit(solution)/shard_map/psum | solution.py:155
  (425 shorter events, 649.9 us)
Async XLA Ops:
  7.2 21.3 %copy-start = (bf16[128,128]{1,0:T(8,128)(2,1)S(1)}, bf16[128,128]{1,0:T(8,128)(2,1)}, u32[]{:S(2)}) copy-start(bf16[128,128]{1,0:T(8,128)(2,1)} %param.19) | copy-start | bytes 98308
  7.2 21.3 %copy-start.1 = (bf16[4096,128]{1,0:T(8,128)(2,1)S(1)}, bf16[4096,128]{1,0:T(8,128)(2,1)}, u32[]{:S(2)}) copy-start(bf16[4096,128]{1,0:T(8,128)(2,1)} %param.16) | copy-start | bytes 3145732
  7.2 879.0 %reduce-scatter.2.cloned.1.call-start = ((), (), s32[]{:S(2)}) async-start(), calls=%async_computation.1 | async-start | bytes 294912 | tf_op jit(solution)/shard_map/reduce_scatter | solution.py:156
  15.4 30.2 %collective-permute-start = (bf16[256]{0:T(256)(128)(2,1)}, bf16[256]{0:T(256)(128)(2,1)}, u32[]{:S(2)}, u32[]{:S(2)}) collective-permute-start(bf16[256]{0:T(256)(128)(2,1)} %get-tuple-element.226), channel_id=1, source_target_pairs={{16,0},{24,8},{32,16},{40,24},{48,32},{56,40},{64,48},{72,56},{80,... | collective-permute-start | bytes 1544 | tf_op jit(solution)/shard_map/ppermute | solution.py:18
  16.7 30.8 %collective-permute-start.1 = (bf16[256]{0:T(256)(128)(2,1)S(1)}, bf16[256]{0:T(256)(128)(2,1)}, u32[]{:S(2)}, u32[]{:S(2)}) collective-permute-start(bf16[256]{0:T(256)(128)(2,1)S(1)} %get-tuple-element.225), channel_id=1, source_target_pairs={{8,0},{16,8},{24,16},{32,24},{40,32},{48,40},{56,48},{64,56},{72,6... | collective-permute-start | bytes 1544 | tf_op jit(solution)/shard_map/ppermute | solution.py:18
  18.0 34.7 %collective-permute-start.2 = (bf16[256]{0:T(256)(128)(2,1)S(1)}, bf16[256]{0:T(256)(128)(2,1)}, u32[]{:S(2)}, u32[]{:S(2)}) collective-permute-start(bf16[256]{0:T(256)(128)(2,1)S(1)} %get-tuple-element.227), channel_id=1, source_target_pairs={{0,8},{8,16},{16,24},{24,32},{32,40},{40,48},{48,56},{56,64},{64,7... | collective-permute-start | bytes 1544 | tf_op jit(solution)/shard_map/ppermute | solution.py:18
  23.1 35.7 %collective-permute-start.3 = (bf16[256]{0:T(256)(128)(2,1)S(1)}, bf16[256]{0:T(256)(128)(2,1)}, u32[]{:S(2)}, u32[]{:S(2)}) collective-permute-start(bf16[256]{0:T(256)(128)(2,1)S(1)} %get-tuple-element.224), channel_id=1, source_target_pairs={{0,16},{8,24},{16,32},{24,40},{32,48},{40,56},{48,64},{56,72},{64,... | collective-permute-start | bytes 1544 | tf_op jit(solution)/shard_map/ppermute | solution.py:18
  28.9 6.6 copy-start.2
  28.9 13.1 %copy-start.6 = (f32[3,128]{1,0:T(4,128)S(1)}, f32[3,128]{1,0:T(4,128)}, u32[]{:S(2)}) copy-start(f32[3,128]{1,0:T(4,128)} %param.22) | copy-start | bytes 4612
  33.3 9.3 copy-start.5
  34.2 51.9 %collective-permute-start.8 = (bf16[256,128]{1,0:T(8,128)(2,1)S(1)}, bf16[256,128]{1,0:T(8,128)(2,1)S(1)}, u32[]{:S(2)}, u32[]{:S(2)}) collective-permute-start(bf16[256,128]{1,0:T(8,128)(2,1)S(1)} %get-tuple-element.213), channel_id=1, source_target_pairs={{16,0},{24,8},{32,16},{40,24},{48,32},{56,40},{64,48},{72,56},{80,... | collective-permute-start | bytes 196616 | tf_op jit(solution)/shard_map/ppermute | solution.py:18
  45.6 40.5 %collective-permute-start.9 = (bf16[256,128]{1,0:T(8,128)(2,1)S(1)}, bf16[256,128]{1,0:T(8,128)(2,1)S(1)}, u32[]{:S(2)}, u32[]{:S(2)}) collective-permute-start(bf16[256,128]{1,0:T(8,128)(2,1)S(1)} %get-tuple-element.212), channel_id=1, source_target_pairs={{8,0},{16,8},{24,16},{32,24},{40,32},{48,40},{56,48},{64,56},{72,6... | collective-permute-start | bytes 196616 | tf_op jit(solution)/shard_map/ppermute | solution.py:18
  47.5 38.6 %collective-permute-start.10 = (bf16[256,128]{1,0:T(8,128)(2,1)S(1)}, bf16[256,128]{1,0:T(8,128)(2,1)S(1)}, u32[]{:S(2)}, u32[]{:S(2)}) collective-permute-start(bf16[256,128]{1,0:T(8,128)(2,1)S(1)} %get-tuple-element.211), channel_id=1, source_target_pairs={{0,8},{8,16},{16,24},{24,32},{32,40},{40,48},{48,56},{56,64},{64,7... | collective-permute-start | bytes 196616 | tf_op jit(solution)/shard_map/ppermute | solution.py:18
  52.7 33.5 %collective-permute-start.11 = (bf16[256,128]{1,0:T(8,128)(2,1)S(1)}, bf16[256,128]{1,0:T(8,128)(2,1)S(1)}, u32[]{:S(2)}, u32[]{:S(2)}) collective-permute-start(bf16[256,128]{1,0:T(8,128)(2,1)S(1)} %get-tuple-element.210), channel_id=1, source_target_pairs={{0,16},{8,24},{16,32},{24,40},{32,48},{40,56},{48,64},{56,72},{64,... | collective-permute-start | bytes 196616 | tf_op jit(solution)/shard_map/ppermute | solution.py:18
  58.8 7.3 collective-permute-start.4
  66.1 5.5 collective-permute-start.5
  71.6 5.8 collective-permute-start.6
  77.4 8.7 collective-permute-start.7
  86.1 0.6 copy-start.4
  814.9 2.4 copy-start.8
  814.9 2.4 copy-start.9
  814.9 2.4 copy-start.10
  820.8 1.2 copy-start.3
  820.8 1.2 copy-start.7
Sparse Core Ops, SparseCore 0:
  848.2 37.9 reduce-scatter.1
where the time goes:
time: 1050 us; the launch traced here: 1040 us
  other arithmetic  347 us (33%)
  local copies, waits for them, and re-layouts  227 us (22%)
  matrix products  214 us (20%)
  blocking collectives  143 us (14%)
  waiting for transfers between devices  48.8 us (5%)
  starting transfers between devices  40.3 us (4%)
  between operations  14.4 us (1%)
    psum x1, blocking collectives, shards(): summed = lax.psum(partial_value.astype(jnp.bfloat16), 'space')  143 us
    dot_general x20, matrix products, tile_terms(): jnp.einsum('gij,gcj->gci', weight, send_pos, precision=lax.Precision.HIGH...  124 us
    scatter-add x20, other arithmetic, tile_terms(): message = message.at[receiver].add(terms)  93.4 us
    dot_general x20, matrix products, tile_terms(): jnp.einsum('gij,gjd->gid', weight.astype(jnp.bfloat16), ext_values[sender...  84.6 us
    reduce_sum x20, other arithmetic, tile_terms(): weight_sum = weight_sum.at[receiver].add(jnp.sum(weight, axis=2))  81.6 us
    scatter-add x20, other arithmetic, tile_terms(): moment.at[receiver]  79.9 us
    slice x40, local copies, waits for them, and re-layouts, tile_terms(): delta = recv_pos[:, c, :, None] - send_pos[:, c, None, :]  64.4 us
    gather x20, local copies, waits for them, and re-layouts, tile_terms(): send_pos = ext_pos[sender]  42.3 us
  transfers between devices with their start and end apart: 13, of which 5 were waited for; matrix products, arithmetic and copies ran while one was open for 2% of the time, Pallas kernels for 0%

commit v1 on v0

--- a/solution.py
+++ b/solution.py
@@ -152,7 +152,7 @@
     partial_value = jax.ops.segment_sum(
         updated.astype(jnp.float32), frag_ids, num_segments=num_frags
     )
-    summed = lax.psum(partial_value.astype(jnp.bfloat16), "space")
+    summed = jnp.sum(lax.all_gather(partial_value.astype(jnp.bfloat16), "space"), axis=0)
     pooled = lax.psum_scatter(summed, "frag", scatter_dimension=0, tiled=True).astype(jnp.float32)
     return (updated, pooled * pool_scale)
 

time: 1050 us -> 1010 us (0.962)
  blocking collectives: 143 us -> 0 us
  waiting for transfers between devices: 48.8 us -> 144 us
    psum x1 -> x0, blocking collectives: 143 us -> none  [shards(): summed = lax.psum(partial_value.astype(jnp.bfloat16), 'space')]
    all_gather x0 -> x1, waiting for transfers between devices: none -> 103 us  [shards(): lax.all_gather(partial_value.astype(jnp.bfloat16), 'space')]
  transfers between devices with their start and end apart: 13 -> 14, of which waited for: 5 -> 6; matrix products, arithmetic and copies ran while one was open for 2% -> 2% of each run, Pallas kernels for 0% -> 0%
where the time goes in v1:
time: 1010 us; the launch traced here: 995 us
  other arithmetic  354 us (35%)
  local copies, waits for them, and re-layouts  228 us (23%)
  matrix products  214 us (21%)
  waiting for transfers between devices  144 us (14%)
  starting transfers between devices  40.4 us (4%)
  between operations  14.4 us (1%)
    dot_general x20, matrix products, tile_terms(): jnp.einsum('gij,gcj->gci', weight, send_pos, precision=lax.Precision.HIGH...  124 us
    all_gather x1, waiting for transfers between devices, shards(): lax.all_gather(partial_value.astype(jnp.bfloat16), 'space')  103 us
    scatter-add x20, other arithmetic, tile_terms(): message = message.at[receiver].add(terms)  93.4 us
    dot_general x20, matrix products, tile_terms(): jnp.einsum('gij,gjd->gid', weight.astype(jnp.bfloat16), ext_values[sender...  84.3 us
    reduce_sum x20, other arithmetic, tile_terms(): weight_sum = weight_sum.at[receiver].add(jnp.sum(weight, axis=2))  81.3 us
    scatter-add x20, other arithmetic, tile_terms(): moment.at[receiver]  79.9 us
    slice x40, local copies, waits for them, and re-layouts, tile_terms(): delta = recv_pos[:, c, :, None] - send_pos[:, c, None, :]  64.7 us
    gather x20, local copies, waits for them, and re-layouts, tile_terms(): send_pos = ext_pos[sender]  42.1 us
  transfers between devices with their start and end apart: 14, of which 6 were waited for; matrix products, arithmetic and copies ran while one was open for 2% of the time, Pallas kernels for 0%

profile of v1, /device:TPU:0, one launch (start us, length us, event | category | flops | bytes accessed | tf_op | source)
XLA Modules:
  0.0 995.3 jit_solution(6783288206476245829)
XLA Ops:
  8.7 6.1 gather_fusion.4
  18.0 5.1 collective-permute-start.2
  23.1 5.4 collective-permute-start.3
  52.7 5.4 collective-permute-start.11
  60.7 5.4 collective-permute-done.4
  77.5 7.6 collective-permute-start.7
  87.0 727.6 %while.17 = (s32[]{:T(128)}, f32[32,128,128]{2,1,0:T(8,128)S(1)}, f32[32,3,128]{2,1,0:T(4,128)}, f32[32,128]{1,0:T(8,128)S(1)}, s32[2,640]{1,0:T(2,128)}, /*inde...) while((s32[]{:T(128)}, f32[32,128,128]{2,1,0:T(8,128)S(1)}, ...), condition=%wide.region_5.0_spmd, body=%wide.region_0.0_spmd.sunk | while | flops 170412320 | bytes 12668991 | solution.py:133
  108.2 6.2 fusion.74
  144.6 6.2 fusion.74
  181.0 6.2 fusion.74
  217.4 6.2 fusion.74
  253.7 6.2 fusion.74
  290.1 6.2 fusion.74
  326.5 6.2 fusion.74
  362.9 6.2 fusion.74
  399.3 6.2 fusion.74
  435.6 6.2 fusion.74
  467.3 4.7 scatter_fusion
  472.0 6.2 fusion.74
  508.4 6.2 fusion.74
  544.8 6.2 fusion.74
  581.2 6.2 fusion.74
  617.5 6.2 fusion.74
  653.9 6.2 fusion.74
  690.3 6.2 fusion.74
  726.7 6.2 fusion.74
  763.1 6.2 fusion.74
  799.4 6.2 fusion.74
  822.8 23.2 %scatter_custom_fusion.3 = f32[1024,128]{1,0:T(8,128)} fusion(s32[4096]{0:T(1024)} %param.29, f32[4096,128]{1,0:T(8,128)S(1)} %copy.23, f32[]{:T(128)} %constant.63.clone.1), kind=kCustom, calls=%fused_computation.58 | custom fusion | flops 524288 | bytes 524800 | tf_op jit(solution)/shard_map/scatter-add | solution.py:152
  847.9 103.5 %all-gather.3.cloned.1.call-done = bf16[32768,128]{1,0:T(8,128)(2,1)} async-done(((bf16[1024,128]{1,0:T(8,128)(2,1)}), bf16[32768,128]{1,0:T(8,128)(2,1)}) %all-gather.3.cloned.1.call-update) | async-done | bytes 8388624 | tf_op jit(solution)/shard_map/all_gather | solution.py:155
  951.4 5.5 reduce_sum.45
  958.2 28.9 %reduce-scatter.2.cloned.1.call-done = bf16[128,128]{1,0:T(8,128)(2,1)} async-done(((bf16[1024,128]{1,0:T(8,128)(2,1)}), bf16[128,128]{1,0:T(8,128)(2,1)}) %reduce-scatter.2.cloned.1.call-update) | async-done | bytes 32784 | tf_op jit(solution)/shard_map/reduce_scatter | solution.py:156
  (428 shorter events, 655.2 us)
Async XLA Ops:
  7.2 21.3 %copy-start = (bf16[128,128]{1,0:T(8,128)(2,1)S(1)}, bf16[128,128]{1,0:T(8,128)(2,1)}, u32[]{:S(2)}) copy-start(bf16[128,128]{1,0:T(8,128)(2,1)} %param.19) | copy-start | bytes 98308
  7.2 21.3 %copy-start.1 = (bf16[4096,128]{1,0:T(8,128)(2,1)S(1)}, bf16[4096,128]{1,0:T(8,128)(2,1)}, u32[]{:S(2)}) copy-start(bf16[4096,128]{1,0:T(8,128)(2,1)} %param.16) | copy-start | bytes 3145732
  7.2 944.2 %all-gather.3.cloned.1.call-start = ((), (), s32[]{:S(2)}) async-start(), calls=%async_computation.2 | async-start | bytes 8650752 | tf_op jit(solution)/shard_map/all_gather | solution.py:155
  15.4 30.3 %collective-permute-start = (bf16[256]{0:T(256)(128)(2,1)}, bf16[256]{0:T(256)(128)(2,1)}, u32[]{:S(2)}, u32[]{:S(2)}) collective-permute-start(bf16[256]{0:T(256)(128)(2,1)} %get-tuple-element.226), channel_id=1, source_target_pairs={{16,0},{24,8},{32,16},{40,24},{48,32},{56,40},{64,48},{72,56},{80,... | collective-permute-start | bytes 1544 | tf_op jit(solution)/shard_map/ppermute | solution.py:18
  16.7 30.9 %collective-permute-start.1 = (bf16[256]{0:T(256)(128)(2,1)S(1)}, bf16[256]{0:T(256)(128)(2,1)}, u32[]{:S(2)}, u32[]{:S(2)}) collective-permute-start(bf16[256]{0:T(256)(128)(2,1)S(1)} %get-tuple-element.225), channel_id=1, source_target_pairs={{8,0},{16,8},{24,16},{32,24},{40,32},{48,40},{56,48},{64,56},{72,6... | collective-permute-start | bytes 1544 | tf_op jit(solution)/shard_map/ppermute | solution.py:18
  18.0 34.8 %collective-permute-start.2 = (bf16[256]{0:T(256)(128)(2,1)S(1)}, bf16[256]{0:T(256)(128)(2,1)}, u32[]{:S(2)}, u32[]{:S(2)}) collective-permute-start(bf16[256]{0:T(256)(128)(2,1)S(1)} %get-tuple-element.227), channel_id=1, source_target_pairs={{0,8},{8,16},{16,24},{24,32},{32,40},{40,48},{48,56},{56,64},{64,7... | collective-permute-start | bytes 1544 | tf_op jit(solution)/shard_map/ppermute | solution.py:18
  23.1 35.8 %collective-permute-start.3 = (bf16[256]{0:T(256)(128)(2,1)S(1)}, bf16[256]{0:T(256)(128)(2,1)}, u32[]{:S(2)}, u32[]{:S(2)}) collective-permute-start(bf16[256]{0:T(256)(128)(2,1)S(1)} %get-tuple-element.224), channel_id=1, source_target_pairs={{0,16},{8,24},{16,32},{24,40},{32,48},{40,56},{48,64},{56,72},{64,... | collective-permute-start | bytes 1544 | tf_op jit(solution)/shard_map/ppermute | solution.py:18
  28.9 6.6 copy-start.2
  28.9 13.1 %copy-start.6 = (f32[3,128]{1,0:T(4,128)S(1)}, f32[3,128]{1,0:T(4,128)}, u32[]{:S(2)}) copy-start(f32[3,128]{1,0:T(4,128)} %param.22) | copy-start | bytes 4612
  33.2 9.3 copy-start.5
  34.2 51.9 %collective-permute-start.8 = (bf16[256,128]{1,0:T(8,128)(2,1)S(1)}, bf16[256,128]{1,0:T(8,128)(2,1)S(1)}, u32[]{:S(2)}, u32[]{:S(2)}) collective-permute-start(bf16[256,128]{1,0:T(8,128)(2,1)S(1)} %get-tuple-element.213), channel_id=1, source_target_pairs={{16,0},{24,8},{32,16},{40,24},{48,32},{56,40},{64,48},{72,56},{80,... | collective-permute-start | bytes 196616 | tf_op jit(solution)/shard_map/ppermute | solution.py:18
  45.6 40.5 %collective-permute-start.9 = (bf16[256,128]{1,0:T(8,128)(2,1)S(1)}, bf16[256,128]{1,0:T(8,128)(2,1)S(1)}, u32[]{:S(2)}, u32[]{:S(2)}) collective-permute-start(bf16[256,128]{1,0:T(8,128)(2,1)S(1)} %get-tuple-element.212), channel_id=1, source_target_pairs={{8,0},{16,8},{24,16},{32,24},{40,32},{48,40},{56,48},{64,56},{72,6... | collective-permute-start | bytes 196616 | tf_op jit(solution)/shard_map/ppermute | solution.py:18
  47.5 38.7 %collective-permute-start.10 = (bf16[256,128]{1,0:T(8,128)(2,1)S(1)}, bf16[256,128]{1,0:T(8,128)(2,1)S(1)}, u32[]{:S(2)}, u32[]{:S(2)}) collective-permute-start(bf16[256,128]{1,0:T(8,128)(2,1)S(1)} %get-tuple-element.211), channel_id=1, source_target_pairs={{0,8},{8,16},{16,24},{24,32},{32,40},{40,48},{48,56},{56,64},{64,7... | collective-permute-start | bytes 196616 | tf_op jit(solution)/shard_map/ppermute | solution.py:18
  52.7 33.5 %collective-permute-start.11 = (bf16[256,128]{1,0:T(8,128)(2,1)S(1)}, bf16[256,128]{1,0:T(8,128)(2,1)S(1)}, u32[]{:S(2)}, u32[]{:S(2)}) collective-permute-start(bf16[256,128]{1,0:T(8,128)(2,1)S(1)} %get-tuple-element.210), channel_id=1, source_target_pairs={{0,16},{8,24},{16,32},{24,40},{32,48},{40,56},{48,64},{56,72},{64,... | collective-permute-start | bytes 196616 | tf_op jit(solution)/shard_map/ppermute | solution.py:18
  58.8 7.3 collective-permute-start.4
  66.1 5.5 collective-permute-start.5
  71.6 5.8 collective-permute-start.6
  77.5 8.7 collective-permute-start.7
  86.1 0.6 copy-start.4
  814.6 2.4 copy-start.8
  814.6 2.4 copy-start.9
  814.6 2.4 copy-start.10
  820.6 1.2 copy-start.3
  820.6 1.2 copy-start.7
  847.9 139.2 %reduce-scatter.2.cloned.1.call-start = ((), (), s32[]{:S(2)}) async-start(), calls=%async_computation.1 | async-start | bytes 294912 | tf_op jit(solution)/shard_map/reduce_scatter | solution.py:156
Sparse Core Ops, SparseCore 0:
  848.0 103.3 all-gather.2
  957.0 30.0 reduce-scatter.1
